TPU v7x, 256 devices: a whole 4x4x8 slice. The times are simulated.
256 devices in a mesh: rep: 4 (over y_lo, core), seq: 64 (over x, z, y_hi).
Axes of the slice: x: 4, y: 4 (y_hi: 2, y_lo: 2; y = y_hi * 2 + y_lo), z: 8, core: 2. Of those that a mesh axis runs over, the one named last changes fastest.
Arguments:
- inputs: bfloat16 [4, 8192, 4096], P('rep', 'seq'), may hold values from -8 to 8
- queries: bfloat16 [4, 8192, 2048], P('rep', 'seq'), may hold values from -4.5 to 4.5
- key_heads: bfloat16 [4, 8192, 512], P('rep', 'seq'), may hold values from -4.5 to 4.5
- cotangent: bfloat16 [4, 8192, 2048], P('rep', 'seq'), may hold values from -6 to 6
- value_weight: float32 [4, 4096, 512], P('rep', 'seq'), may hold values from -6 to 6
- random_blocks: int32 [64, 2], replicated, may hold values from 0 to 63, as said below
Outputs:
- input_grad: bfloat16 [4, 8192, 4096], P('rep', 'seq')
- query_gradient: bfloat16 [4, 8192, 2048], P('rep', 'seq')
- key_grad: bfloat16 [4, 8192, 512], P('rep', 'seq')
- new_weight: float32 [4, 4096, 512], P('rep', 'seq')
Inputs may be any that keep to these rules, and one draw needn't show every extreme that they name: Device k of seq holds block k; let n = 64. For each slot j there is one offset o_j for all blocks, with o_0 + o_1 = n - 1 and both at least 1, such that random_blocks[i, j] = (i - o_j) mod n.
All inputs are finite; a program needn't handle non-finite values.
Results may differ from a plain program's by a relative error of at most 0.012.
Values may be sent and summed in bfloat16 or wider, within the bound.
A program may use at most 128 MiB of HBM per device.

v0:
```python
import jax
import jax.numpy as jnp
from jax import lax
from jax.sharding import PartitionSpec as P

HEADS = 16
KV_HEADS = 4
HD = 128
BLOCK_TOKENS = 128
RAND = 2
STEP = 4
KEY_BLOCK_COUNT = 6


learn_rate = 2.0
masked_score = -1e30


def shifted(block, axis, distance):
    devices = range(lax.axis_size(axis))
    route = [((i - distance) % len(devices), i) for i in devices]
    return lax.ppermute(block, axis, route)


def broadcast(value, axis, source):
    kept = jnp.where(lax.axis_index(axis) == source, value, 0).astype(value.dtype)
    return lax.psum(kept, axis)


def move_blocks(payload, offset):
    return shifted(payload, "seq", offset)


def section_test(offsets, section_bit):
    return offsets // 2**section_bit % 2 == 1


def carry_far(payload, offsets, section_count, direction):
    for section_bit in range(section_count):
        section_on = section_test(offsets, section_bit)
        arrived = move_blocks(payload, direction * 2**section_bit)
        payload = jnp.where(section_on[:, None, None], arrived, payload)
    return payload


def shards(inputs, queries, key_heads, cotangent, value_weight, random_blocks):
    tokens = inputs[0]
    query_rows = queries[0]
    key_rows = key_heads[0]
    upstream_rows = cotangent[0]
    weight = value_weight[0]
    rows_dev = tokens.shape[0]
    model_width = tokens.shape[1]
    kv_width = key_rows.shape[1]
    q_width = query_rows.shape[1]
    pair_width = 2 * kv_width
    blocks_dev = rows_dev // BLOCK_TOKENS
    heads_group = HEADS // KV_HEADS
    seq_count = lax.axis_size("seq")
    seq_index = lax.axis_index("seq")
    section_count = seq_count.bit_length() - 1
    proj_scale = model_width ** (-0.5)
    score_factor = HD ** (-0.5)
    weight_low = weight.astype(jnp.bfloat16)
    whole_weight = lax.all_gather(weight_low, "seq", axis=0, tiled=True)
    projected = jnp.dot(tokens, whole_weight, preferred_element_type=jnp.float32)
    values = (projected * proj_scale).astype(jnp.bfloat16)
    key_pairs = jnp.concatenate([key_rows, values], axis=1)
    left_rim = move_blocks(key_pairs, 1)
    right_rim = move_blocks(key_pairs, -1)
    global_pairs = broadcast(key_pairs, "seq", 0)
    rand_rows = lax.dynamic_slice_in_dim(random_blocks, seq_index * blocks_dev, blocks_dev, 0)
    offsets = (seq_index - rand_rows[0] // blocks_dev) % seq_count
    chosen_sub = rand_rows % blocks_dev
    far_pairs = carry_far(jnp.stack([key_pairs] * RAND), offsets, section_count, 1)
    far_blocks = far_pairs.reshape(RAND, blocks_dev, BLOCK_TOKENS, pair_width)
    slot_ids = jnp.arange(RAND)
    picked = far_blocks[slot_ids[None, :], chosen_sub]
    beside_all = jnp.concatenate([left_rim, key_pairs, right_rim], axis=0).reshape(
        blocks_dev + 2, BLOCK_TOKENS, pair_width
    )
    global_tile = global_pairs[None, None]
    key_sets = jnp.concatenate(
        [beside_all[:-2, None], beside_all[1:-1, None], beside_all[2:, None], global_tile, picked],
        axis=1,
    )
    block_ids = seq_index * blocks_dev + jnp.arange(blocks_dev)
    left_ok = (block_ids > 0)[:, None]
    right_ok = (block_ids < seq_count * blocks_dev - 1)[:, None]
    present = jnp.concatenate(
        [left_ok, jnp.ones_like(left_ok), right_ok, jnp.ones((blocks_dev, 1 + RAND), bool)], axis=1
    )
    key_mask = jnp.repeat(present, BLOCK_TOKENS, axis=1)
    split_sets = key_sets.reshape(blocks_dev, KEY_BLOCK_COUNT * BLOCK_TOKENS, 2, KV_HEADS, HD)
    key_portion = split_sets[:, :, 0]
    value_portion = split_sets[:, :, 1]
    query_portion = query_rows.reshape(blocks_dev, BLOCK_TOKENS, KV_HEADS, heads_group, HD)
    upstream_portion = upstream_rows.reshape(blocks_dev, BLOCK_TOKENS, KV_HEADS, heads_group, HD)
    score_matrix = (
        jnp.einsum(
            "ptgrd,psgd->pgrts", query_portion, key_portion, preferred_element_type=jnp.float32
        )
        * score_factor
    )
    score_matrix = jnp.where(key_mask[:, None, None, None, :], score_matrix, masked_score)
    highest = jnp.max(score_matrix, axis=-1, keepdims=True)
    exp_scores = jnp.exp(score_matrix - highest)
    soft_weights = exp_scores / jnp.sum(exp_scores, axis=-1, keepdims=True)
    softmax_lowered = soft_weights.astype(jnp.bfloat16)
    attended_output = jnp.einsum(
        "pgrts,psgd->ptgrd", softmax_lowered, value_portion, preferred_element_type=jnp.float32
    )
    row_delta = jnp.sum(upstream_portion.astype(jnp.float32) * attended_output, axis=-1)
    weight_gradient = jnp.einsum(
        "ptgrd,psgd->pgrts", upstream_portion, value_portion, preferred_element_type=jnp.float32
    )
    score_gradient = (
        soft_weights
        * (weight_gradient - jnp.transpose(row_delta, (0, 2, 3, 1))[..., None])
        * score_factor
    ).astype(jnp.bfloat16)
    query_gradient = (
        jnp.einsum(
            "pgrts,psgd->ptgrd", score_gradient, key_portion, preferred_element_type=jnp.float32
        )
        .astype(jnp.bfloat16)
        .reshape(rows_dev, q_width)
    )
    key_delta_rows = jnp.einsum(
        "pgrts,ptgrd->psgd", score_gradient, query_portion, preferred_element_type=jnp.float32
    )
    value_delta_rows = jnp.einsum(
        "pgrts,ptgrd->psgd", softmax_lowered, upstream_portion, preferred_element_type=jnp.float32
    )
    changes = jnp.concatenate(
        [
            key_delta_rows.reshape(blocks_dev, KEY_BLOCK_COUNT, BLOCK_TOKENS, kv_width),
            value_delta_rows.reshape(blocks_dev, KEY_BLOCK_COUNT, BLOCK_TOKENS, kv_width),
        ],
        axis=-1,
    )
    rounded = changes.astype(jnp.bfloat16)
    back_left = move_blocks(rounded[0, 0], -1)
    back_right = move_blocks(rounded[blocks_dev - 1, 2], 1)
    global_sum = lax.psum(jnp.sum(changes[:, 3], axis=0), "seq")
    slot_onehot = jax.nn.one_hot(chosen_sub, blocks_dev, dtype=jnp.bfloat16)
    rand_back = jnp.einsum(
        "pjb,pjtc->jbtc", slot_onehot, rounded[:, 4:], preferred_element_type=jnp.float32
    ).astype(jnp.bfloat16)
    returned = carry_far(rand_back.reshape(RAND, rows_dev, pair_width), offsets, section_count, -1)
    totals = changes[:, 1] + jnp.concatenate([rounded[1:, 0], back_left[None]], axis=0).astype(
        jnp.float32
    )
    totals = totals + jnp.concatenate([back_right[None], rounded[:-1, 2]], axis=0).astype(
        jnp.float32
    )
    totals = totals + jnp.sum(returned.astype(jnp.float32), axis=0).reshape(
        blocks_dev, BLOCK_TOKENS, pair_width
    )
    owner_first = (seq_index == 0) & (jnp.arange(blocks_dev) == 0)
    totals = totals + jnp.where(owner_first[:, None, None], global_sum[None], 0.0)
    key_grad = totals[..., :kv_width].reshape(rows_dev, kv_width).astype(jnp.bfloat16)
    value_total = totals[..., kv_width:].reshape(rows_dev, kv_width).astype(jnp.bfloat16)
    contract_cols = (((1,), (1,)), ((), ()))
    back_proj = lax.dot_general(
        value_total, whole_weight, contract_cols, preferred_element_type=jnp.float32
    )
    input_grad = (back_proj * proj_scale).astype(jnp.bfloat16)
    contract_rows = (((0,), (0,)), ((), ()))
    weight_change = lax.psum_scatter(
        lax.dot_general(tokens, value_total, contract_rows, preferred_element_type=jnp.float32)
        * proj_scale,
        "seq",
        scatter_dimension=0,
        tiled=True,
    )
    updated = weight - learn_rate * weight_change
    rep_sections = lax.axis_size("rep").bit_length() - 1
    peer_weight = shifted(updated.astype(jnp.bfloat16), "rep", 2 ** (STEP % rep_sections)).astype(
        updated.dtype
    )
    new_weight = 0.5 * (updated + peer_weight)
    return (input_grad[None], query_gradient[None], key_grad[None], new_weight[None])


def solution(mesh):
    placed = (
        P("rep", "seq", None),
        P("rep", "seq", None),
        P("rep", "seq", None),
        P("rep", "seq", None),
        P("rep", "seq", None),
        P(),
    )
    return jax.shard_map(
        shards,
        mesh=mesh,
        in_specs=placed,
        out_specs=(
            P("rep", "seq", None),
            P("rep", "seq", None),
            P("rep", "seq", None),
            P("rep", "seq", None),
        ),
        check_vma=False,
    )
```

profile of v0, /device:TPU:1, one launch (start us, length us, event | category | flops | bytes accessed | tf_op | source)
XLA Modules:
  0.0 2109.1 jit_solution(15223461090343345438)
XLA Ops:
  9.0 130.6 %all-gather.2.cloned.1.call-done = bf16[4096,512]{1,0:T(8,128)(2,1)} async-done(((bf16[64,512]{1,0:T(8,128)(2,1)}), bf16[4096,512]{1,0:T(8,128)(2,1)}) %all-gather.2.cloned.1.call-update) | async-done | bytes 4194320 | tf_op jit(solution)/shard_map/all_gather | solution.py:65
  144.5 13.9 collective-permute-done.2
  158.7 11.3 collective-permute-done.3
  170.2 16.4 collective-permute-done.4
  186.9 25.5 %collective-permute-done.5 = bf16[2,128,1024]{2,1,0:T(8,128)(2,1)S(1)} collective-permute-done((bf16[2,128,1024]{2,1,0:T(8,128)(2,1)S(1)}, bf16[2,128,1024]{2,1,0:T(8,128)(2,1)S(1)}, u32[]{:S(2)}, u32[]{:S(2)}) %collective-permute-start.5) | collective-permute-done | bytes 524320 | tf_op jit(solution)/shard_map/ppermute | solution.py:22
  216.8 4.1 collective-permute-start.1
  220.9 3.6 collective-permute-start
  225.0 7.3 collective-permute-done
  236.3 620.2 %all-reduce.3.cloned.1.call-done = bf16[1,1,128,1024]{3,2,1,0:T(8,128)(2,1)} async-done(((bf16[1,1,128,1024]{3,2,1,0:T(8,128)(2,1)}), bf16[1,1,128,1024]{3,2,1,0:T(8,128)(2,1)}) %all-reduce.3.cloned.1.call-update) | async-done | bytes 262160 | tf_op jit(solution)/shard_map/psum | solution.py:27
  893.5 6.8 collective-permute-done.10
  901.4 7.1 collective-permute-done.11
  909.4 10.1 collective-permute-done.12
  919.6 14.4 collective-permute-start.13
  934.0 8.1 collective-permute-done.13
  942.3 8.2 collective-permute-done.14
  952.4 14.6 collective-permute-start.8
  968.6 10.8 collective-permute-done.8
  979.4 9.4 collective-permute-done.9
  988.9 664.4 %all-reduce.5.cloned.1.call-done = f32[128,1024]{1,0:T(8,128)} async-done(((f32[128,1024]{1,0:T(8,128)}), f32[128,1024]{1,0:T(8,128)}) %all-reduce.5.cloned.1.call-update) | async-done | bytes 524304 | tf_op jit(solution)/shard_map/psum | solution.py:145
  1654.7 4.5 multiply_bitcast_fusion
  1659.2 9.1 copy.53
  1671.9 372.6 %reduce-scatter.4.cloned.1.call-done = f32[64,512]{1,0:T(8,128)} async-done(((f32[4096,512]{1,0:T(8,128)}), f32[64,512]{1,0:T(8,128)}) %reduce-scatter.4.cloned.1.call-update) | async-done | bytes 131088 | tf_op jit(solution)/shard_map/reduce_scatter | solution.py:170
  2045.5 51.1 %collective-permute-start.16 = (bf16[64,512]{1,0:T(8,128)(2,1)S(1)}, bf16[64,512]{1,0:T(8,128)(2,1)S(1)}, u32[]{:S(2)}, u32[]{:S(2)}) collective-permute-start(bf16[64,512]{1,0:T(8,128)(2,1)S(1)} %fusion.40), channel_id=1, source_target_pairs={{192,0},{0,64},{64,128},{128,192},{193,1},{1,65},{65,129},{129,193... | collective-permute-start | bytes 196616 | tf_op jit(solution)/shard_map/ppermute | solution.py:22
  2096.6 4.6 fusion.7
  (115 shorter events, 66.1 us)
Async XLA Ops:
  7.2 135.3 %copy-start.11 = (bf16[1,128,512]{2,1,0:T(8,128)(2,1)S(1)}, bf16[1,128,512]{2,1,0:T(8,128)(2,1)}, u32[]{:S(2)}) copy-start(bf16[1,128,512]{2,1,0:T(8,128)(2,1)} %param.8) | copy-start | bytes 393220
  7.2 136.6 %copy-start.15 = (s32[64,2]{0,1:T(2,128)S(1)}, s32[64,2]{0,1:T(2,128)}, u32[]{:S(2)}) copy-start(s32[64,2]{0,1:T(2,128)} %param.11) | copy-start | bytes 1540
  7.2 132.4 %all-gather.2.cloned.1.call-start = ((), (), s32[]{:S(2)}) async-start(), calls=%async_computation.1 | async-start | bytes 4259840 | tf_op jit(solution)/shard_map/all_gather | solution.py:65
  8.9 847.6 %all-reduce.3.cloned.1.call-start = ((), (), s32[]{:S(2)}) async-start(), calls=%async_computation.2 | async-start | bytes 524288 | tf_op jit(solution)/shard_map/psum | solution.py:27
  143.4 15.0 collective-permute-start.2
  158.6 11.4 collective-permute-start.3
  170.2 16.5 collective-permute-start.4
  186.8 25.5 %collective-permute-start.5 = (bf16[2,128,1024]{2,1,0:T(8,128)(2,1)S(1)}, bf16[2,128,1024]{2,1,0:T(8,128)(2,1)S(1)}, u32[]{:S(2)}, u32[]{:S(2)}) collective-permute-start(bf16[2,128,1024]{2,1,0:T(8,128)(2,1)S(1)} %broadcast_select_fusion.5), channel_id=1, source_target_pairs={{56,0},{57,1},{58,2},{59,3},{60,4},{61,5},{62,6},{63,7},{0,8},{1,9... | collective-permute-start | bytes 1572872 | tf_op jit(solution)/shard_map/ppermute | solution.py:22
  212.5 12.1 collective-permute-start.6
  216.8 18.7 collective-permute-start.1
  220.9 11.4 collective-permute-start
  224.5 1428.8 %all-reduce.5.cloned.1.call-start = ((), (), s32[]{:S(2)}) async-start(), calls=%async_computation.3 | async-start | bytes 1048576 | tf_op jit(solution)/shard_map/psum | solution.py:145
  224.7 633.5 %collective-permute-start.7 = (bf16[2,128,1024]{2,1,0:T(8,128)(2,1)S(1)}, bf16[2,128,1024]{2,1,0:T(8,128)(2,1)S(1)}, u32[]{:S(2)}, u32[]{:S(2)}) collective-permute-start(bf16[2,128,1024]{2,1,0:T(8,128)(2,1)S(1)} %broadcast_select_fusion.9), channel_id=1, source_target_pairs={{32,0},{33,1},{34,2},{35,3},{36,4},{37,5},{38,6},{39,7},{40,8},{41... | collective-permute-start | bytes 1572872 | tf_op jit(solution)/shard_map/ppermute | solution.py:22
  890.7 9.6 collective-permute-start.10
  900.4 8.1 collective-permute-start.11
  908.7 10.8 collective-permute-start.12
  919.6 22.5 %collective-permute-start.13 = (bf16[2,128,1024]{2,1,0:T(8,128)(2,1)S(1)}, bf16[2,128,1024]{2,1,0:T(8,128)(2,1)S(1)}, u32[]{:S(2)}, u32[]{:S(2)}) collective-permute-start(bf16[2,128,1024]{2,1,0:T(8,128)(2,1)S(1)} %broadcast_select_fusion.4), channel_id=1, source_target_pairs={{8,0},{9,1},{10,2},{11,3},{12,4},{13,5},{14,6},{15,7},{16,8},{17,9... | collective-permute-start | bytes 1572872 | tf_op jit(solution)/shard_map/ppermute | solution.py:22
  942.2 8.3 collective-permute-start.14
  951.4 15.6 collective-permute-start.15
  952.3 1092.2 %reduce-scatter.4.cloned.1.call-start = ((), (), s32[]{:S(2)}) async-start(), calls=%async_computation.4 | async-start | bytes 8519680 | tf_op jit(solution)/shard_map/reduce_scatter | solution.py:170
  952.4 27.0 %collective-permute-start.8 = (bf16[128,1024]{1,0:T(8,128)(2,1)S(1)}, bf16[128,1024]{1,0:T(8,128)(2,1)S(1)}, u32[]{:S(2)}, u32[]{:S(2)}) collective-permute-start(bf16[128,1024]{1,0:T(8,128)(2,1)S(1)} %get-tuple-element.14), channel_id=1, source_target_pairs={{1,0},{2,1},{3,2},{4,3},{5,4},{6,5},{7,6},{8,7},{9,8},{10,9},{11,1... | collective-permute-start | bytes 786440 | tf_op jit(solution)/shard_map/ppermute | solution.py:22
  967.0 21.8 %collective-permute-start.9 = (bf16[128,1024]{1,0:T(8,128)(2,1)S(1)}, bf16[128,1024]{1,0:T(8,128)(2,1)S(1)}, u32[]{:S(2)}, u32[]{:S(2)}) collective-permute-start(bf16[128,1024]{1,0:T(8,128)(2,1)S(1)} %get-tuple-element.15), channel_id=1, source_target_pairs={{63,0},{0,1},{1,2},{2,3},{3,4},{4,5},{5,6},{6,7},{7,8},{8,9},{9,10... | collective-permute-start | bytes 786440 | tf_op jit(solution)/shard_map/ppermute | solution.py:22
  1668.3 376.2 %copy-start.6 = (f32[1,64,512]{2,1,0:T(8,128)S(1)}, f32[1,64,512]{2,1,0:T(8,128)}, u32[]{:S(2)}) copy-start(f32[1,64,512]{2,1,0:T(8,128)} %param.10) | copy-start | bytes 393220
  2045.5 56.4 %collective-permute-start.16 = (bf16[64,512]{1,0:T(8,128)(2,1)S(1)}, bf16[64,512]{1,0:T(8,128)(2,1)S(1)}, u32[]{:S(2)}, u32[]{:S(2)}) collective-permute-start(bf16[64,512]{1,0:T(8,128)(2,1)S(1)} %fusion.40), channel_id=1, source_target_pairs={{192,0},{0,64},{64,128},{128,192},{193,1},{1,65},{65,129},{129,193... | collective-permute-start | bytes 196616 | tf_op jit(solution)/shard_map/ppermute | solution.py:22
  (14 other events, 547.5 us)
Sparse Core Ops, SparseCore 0:
  12.1 127.4 all-gather.1
  224.6 631.8 all-reduce.2
  952.4 700.8 all-reduce.4
  1668.4 376.0 reduce-scatter.3
where the time goes:
time: 2110 us
  waiting for transfers between devices  1920 us (91%)
  starting transfers between devices  93.6 us (4%)
  local copies, waits for them, and re-layouts  38.4 us (2%)
  matrix products  25.7 us (1%)
    psum x1, waiting for transfers between devices, shards(): global_sum = lax.psum(jnp.sum(changes[:, 3], axis=0), 'seq')  664 us
    psum x1, waiting for transfers between devices, broadcast(): return lax.psum(kept, axis)  620 us
    reduce_scatter x1, waiting for transfers between devices, shards(): lax.psum_scatter(lax.dot_general(tokens, value_total, contract_rows, pref...  373 us
    ppermute x17, waiting for transfers between devices, shifted(): return lax.ppermute(block, axis, route)  135 us
    all_gather x1, waiting for transfers between devices, shards(): whole_weight = lax.all_gather(weight_low, 'seq', axis=0, tiled=True)  131 us
    ppermute x17, starting transfers between devices, shifted(): return lax.ppermute(block, axis, route)  93.5 us
  transfers between devices with their start and end apart: 21, of which 16 were waited for; matrix products, arithmetic and copies ran while one was open for 1% of the time, Pallas kernels for 0%

commit v1 on v0

v1 whole, which is shorter than its diff:
```python
import functools
import jax
import jax.numpy as jnp
from jax import lax
from jax.experimental import pallas as pl
from jax.experimental.pallas import tpu as pltpu
from jax.sharding import PartitionSpec as P

HEADS = 16
KV_HEADS = 4
HD = 128
BLOCK_TOKENS = 128
STEP = 4
LEARN_RATE = 2.0
MASKED = -1e30
GROUP = HEADS // KV_HEADS
MESH = pl.DeviceIdType.MESH
F32 = jnp.float32
BF16 = jnp.bfloat16


def grid_of(n):
    return {64: (4, 8), 16: (2, 4), 8: (2, 2)}[n]


class Place:
    def __init__(self, n, send_sem, recv_sem):
        self.n = n
        self.nx, self.nz = grid_of(n)
        self.me = lax.axis_index("seq")
        self.x = self.me // (2 * self.nz)
        self.z = lax.rem(self.me // 2, self.nz)
        self.y = lax.rem(self.me, 2)
        self.send_sem, self.recv_sem = send_sem, recv_sem
        self.taken = 0
        self.started = []

    def at(self, x, z, y):
        return x * (2 * self.nz) + z * 2 + y

    def xs(self, d):
        return lax.rem(self.x + d + self.nx, self.nx)

    def zs(self, d):
        return lax.rem(self.z + d + self.nz, self.nz)

    def slot(self, count=1):
        first = self.taken
        self.taken += count
        return first

    def copy(self, src, dst, target, slot, recv_slot=None, axis="seq"):
        return pltpu.make_async_remote_copy(
            src_ref=src,
            dst_ref=dst,
            send_sem=self.send_sem.at[slot],
            recv_sem=self.recv_sem.at[slot if recv_slot is None else recv_slot],
            device_id={axis: target},
            device_id_type=MESH,
        )

    def send(self, src, dst, target, slot, axis="seq"):
        made = self.copy(src, dst, target, slot, axis=axis)
        made.start()
        self.started.append(made)
        return made

    def drain(self):
        for made in self.started:
            made.wait_send()
        self.started = []

    def greet(self, near=True, rep=False, first=False):
        barrier = pltpu.get_barrier_semaphore()
        peers = [{"seq": self.at(self.xs(d), self.z, self.y)} for d in range(1, self.nx)]
        peers += [{"seq": self.at(self.x, self.zs(d), self.y)} for d in range(1, self.nz)]
        peers += [{"seq": self.at(self.x, self.z, 1 - self.y)}]
        if near:
            peers += [{"seq": lax.rem(self.me + d, self.n)} for d in (1, self.n - 1)]
        if rep:
            reps = lax.axis_size("rep")
            here = lax.axis_index("rep")
            peers += [{"rep": lax.rem(here + d, reps)} for d in (rep, reps - rep)]
        for peer in peers:
            pl.semaphore_signal(barrier, inc=1, device_id=peer, device_id_type=MESH)
        if first:
            @pl.when(self.me == 0)
            def _():
                for p in range(1, 2 * self.nx):
                    pl.semaphore_signal(
                        barrier, inc=1, device_id={"seq": self.at(p // 2, 0, p % 2)},
                        device_id_type=MESH,
                    )

            @pl.when((self.z == 0) & (self.me != 0))
            def _():
                pl.semaphore_signal(barrier, inc=1, device_id={"seq": 0}, device_id_type=MESH)

        count = len(peers)
        if first:
            more = jnp.where(self.z == 0, 1, 0)
            count = count + jnp.where(self.me == 0, 2 * self.nx - 1, more)
        pl.semaphore_wait(barrier, count)


class Spread:
    def __init__(self, pl_, src, dst):
        self.p, self.src, self.dst = pl_, src, dst
        p = pl_
        self.rows = src.shape[0] // (2 * p.nx)
        self.piece = p.x * 2 + p.y
        self.a = p.slot(2 * p.nx)
        self.b = p.slot(p.nz)
        self.c = p.slot()
        self.d = p.slot(p.nx)

    def cut(self, ref, index, rows=None):
        rows = rows or self.rows
        return ref.at[pl.ds(pl.multiple_of(index * rows, rows), rows)]

    def one(self, p):
        first = []
        for i in range(1, 2 * p.nx):
            first.append(
                p.copy(
                    self.src.at[pl.ds(i * self.rows, self.rows)],
                    self.dst.at[pl.ds(i * self.rows, self.rows)],
                    p.at(i // 2, 0, i % 2), self.a + i, self.a,
                )
            )

        @pl.when(p.me == 0)
        def _():
            for made in first:
                made.start()
            self.dst[pl.ds(0, self.rows)] = self.src[pl.ds(0, self.rows)]
        self.first = first

    def two(self, p):
        mine = self.cut(self.dst, self.piece)
        second = [
            p.copy(mine, mine, p.at(p.x, d, p.y), self.b + d, self.b) for d in range(1, p.nz)
        ]

        @pl.when((p.z == 0) & (p.me != 0))
        def _():
            self.first[0].wait_recv()

        @pl.when(p.z == 0)
        def _():
            for made in second:
                made.start()
        self.second = second

    def three(self, p):
        mine = self.cut(self.dst, self.piece)

        @pl.when(p.z != 0)
        def _():
            self.second[0].wait_recv()
        self.third = p.send(mine, mine, p.at(p.x, p.z, 1 - p.y), self.c)

    def four(self, p):
        self.third.wait_recv()
        pair = self.cut(self.dst, p.x, 2 * self.rows)
        self.fourth = [
            p.send(pair, pair, p.at(p.xs(d), p.z, p.y), self.d + d) for d in range(1, p.nx)
        ]

    def end(self, p):
        for made in self.fourth:
            made.wait_recv()

        @pl.when(p.me == 0)
        def _():
            for made in self.first:
                made.wait_send()

        @pl.when(p.z == 0)
        def _():
            for made in self.second:
                made.wait_send()


def gather_kernel(n, scale, tok, key, wl, kv, wk, tt, pbuf, rbuf, send_sem, recv_sem):
    p = Place(n, send_sem, recv_sem)
    nx, nz = p.nx, p.nz
    width = tok.shape[1] // nx
    half = nz // 2
    p.greet(first=True)

    right = p.at(p.x, p.zs(1), p.y)
    left = p.at(p.x, p.zs(-1), p.y)
    after = lax.rem(p.me + 1, n)
    before = lax.rem(p.me + n - 1, n)

    def shard(dz, k):
        return p.zs(dz) * 2 + (p.y if k == 0 else 1 - p.y)

    rs = [[p.slot() for _ in range(2)] for _ in range(half)]
    ls = [[p.slot() for _ in range(2)] for _ in range(half)]

    def relay(s, k):
        out = []
        src_r = wl if (s == 0 and k == 0) else wk.at[shard(-s, k)]
        src_l = wl if (s == 0 and k == 0) else wk.at[shard(s, k)]
        if s < half - 1 or k == 0:
            hops_r[s][k] = p.send(src_r, wk.at[shard(-s, k)], right, rs[s][k])
        if s < half - 1 or k == 1:
            hops_l[s][k] = p.send(src_l, wk.at[shard(s, k)], left, ls[s][k])

    hops_r = [[None, None] for _ in range(half)]
    hops_l = [[None, None] for _ in range(half)]

    other = p.send(wl, wk.at[shard(0, 0)], p.at(p.x, p.z, 1 - p.y), p.slot())
    relay(0, 0)
    cols = [p.slot() for _ in range(nx)]
    moved = []
    for d in range(1, nx):
        to = p.xs(d)
        part = tok.at[:, pl.ds(pl.multiple_of(to * width, width), width)]
        moved.append(p.send(part, tt.at[p.x], p.at(to, p.z, p.y), cols[d]))
    key_right = p.send(key, kv.at[0, 0], after, p.slot())
    key_left = p.send(key, kv.at[2, 0], before, p.slot())
    keys0 = Spread(p, key, kv.at[3, 0])
    keys0.one(p)
    kv[1, 0] = key[...]
    wk[shard(0, 0)] = wl[...]
    tt[p.x] = tok[:, pl.ds(pl.multiple_of(p.x * width, width), width)]
    other.wait_recv()
    relay(0, 1)
    stages = [keys0.two, keys0.three, keys0.four]
    for s in range(1, half):
        for k in range(2):
            if hops_r[s - 1][k] is not None:
                hops_r[s - 1][k].wait_recv()
            if hops_l[s - 1][k] is not None:
                hops_l[s - 1][k].wait_recv()
            relay(s, k)
        if stages:
            stages.pop(0)(p)
    while stages:
        stages.pop(0)(p)
    for k in range(2):
        if hops_r[half - 1][k] is not None:
            hops_r[half - 1][k].wait_recv()
        if hops_l[half - 1][k] is not None:
            hops_l[half - 1][k].wait_recv()
    for made in moved:
        made.wait_recv()
    weight = wk[...].reshape(2 * nz * wk.shape[1], wk.shape[2])
    sums = [p.slot() for _ in range(nx)]
    parts = []
    for d in range(1, nx):
        to = p.xs(d)
        part = jnp.dot(tt[to], weight, preferred_element_type=F32) * scale
        pbuf[to] = part.astype(BF16)
        parts.append(p.send(pbuf.at[to], rbuf.at[p.x], p.at(to, p.z, p.y), sums[d]))
    total = jnp.dot(tt[p.x], weight, preferred_element_type=F32) * scale
    for d in range(1, nx):
        parts[d - 1].wait_recv()
        total = total + rbuf[p.xs(-d)].astype(F32)
    kv[1, 1] = total.astype(BF16)
    own = kv.at[1, 1]
    val_right = p.send(own, kv.at[0, 1], after, p.slot())
    val_left = p.send(own, kv.at[2, 1], before, p.slot())
    vals0 = Spread(p, own, kv.at[3, 1])
    vals0.one(p)
    vals0.two(p)
    vals0.three(p)
    vals0.four(p)
    keys0.end(p)
    vals0.end(p)
    for made in (key_right, key_left, val_right, val_left):
        made.wait_recv()
    p.drain()


def attend_kernel(
    n, q, cot, kv, ra, rb, dq, tot, cha, chb,
    kc, vc, qs, cs, sc, gw, low, out_l, out_r, out_g, in_l, in_r,
    g1, r1, g2, r2, g3, r3, g4, send_sem, recv_sem,
):
    p = Place(n, send_sem, recv_sem)
    nx, nz = p.nx, p.nz
    p.greet(first=True)
    score = HD ** -0.5
    for s in range(6):
        src = kv.at[s] if s < 4 else (ra, rb)[s - 4]
        kc[s] = src[0]
        vc[s] = src[1]
    first_ok = jnp.where(p.me == 0, MASKED, 0.0)
    last_ok = jnp.where(p.me == n - 1, MASKED, 0.0)
    nt = (((1,), (1,)), ((), ()))
    tn = (((0,), (0,)), ((), ()))
    nn = (((1,), (0,)), ((), ()))

    def mm(a, b, dims):
        return lax.dot_general(a, b, dims, preferred_element_type=F32)

    def group(g, _):
        cols = pl.ds(pl.multiple_of(g * HD, HD), HD)
        for r in range(GROUP):
            head = pl.ds(pl.multiple_of((g * GROUP + r) * HD, HD), HD)
            qs[pl.ds(r * BLOCK_TOKENS, BLOCK_TOKENS)] = q[:, head]
            cs[pl.ds(r * BLOCK_TOKENS, BLOCK_TOKENS)] = cot[:, head]
        high = None
        for s in range(6):
            t = mm(kc[s, :, cols], qs[...], nt) * score
            if s == 0:
                t = t + first_ok
            if s == 2:
                t = t + last_ok
            sc[s] = t
            m = jnp.max(t, axis=0, keepdims=True)
            high = m if high is None else jnp.maximum(high, m)
        total = None
        for s in range(6):
            e = jnp.exp(sc[s] - high)
            sc[s] = e
            m = jnp.sum(e, axis=0, keepdims=True)
            total = m if total is None else total + m
        inv = 1.0 / total
        delta = None
        for s in range(6):
            w = sc[s] * inv
            sc[s] = w
            wl = w.astype(BF16)
            low[s] = wl
            gv = mm(vc[s, :, cols], cs[...], nt)
            gw[s] = gv
            m = jnp.sum(wl.astype(F32) * gv, axis=0, keepdims=True)
            delta = m if delta is None else delta + m
        back = None
        for s in range(6):
            ds = (sc[s] * (gw[s] - delta) * score).astype(BF16)
            dv = mm(low[s], cs[...], nn)
            dk = mm(ds, qs[...], nn)
            if s == 1:
                tot[0, :, cols] = dk
                tot[1, :, cols] = dv
            else:
                to = {0: out_l, 2: out_r, 3: out_g, 4: cha, 5: chb}[s]
                to[0, :, cols] = dk.astype(BF16)
                to[1, :, cols] = dv.astype(BF16)
            part = mm(kc[s, :, cols], ds, tn)
            back = part if back is None else back + part
        for r in range(GROUP):
            head = pl.ds(pl.multiple_of((g * GROUP + r) * HD, HD), HD)
            piece = back[:, r * BLOCK_TOKENS:(r + 1) * BLOCK_TOKENS]
            dq[:, head] = piece.T.astype(BF16)
        return 0

    lax.fori_loop(0, KV_HEADS, group, 0)

    after = lax.rem(p.me + 1, n)
    before = lax.rem(p.me + n - 1, n)
    to_left = p.send(out_l, in_r, before, p.slot())
    to_right = p.send(out_r, in_l, after, p.slot())
    rows = BLOCK_TOKENS // nx
    cut = rows // 2

    def row(index, size):
        return pl.ds(pl.multiple_of(index * size, size), size)

    base = p.slot(nx)
    ones = [
        p.send(out_g.at[:, row(p.xs(d), rows)], g1.at[p.x], p.at(p.xs(d), p.z, p.y), base + d)
        for d in range(1, nx)
    ]
    acc = out_g[:, row(p.x, rows)].astype(F32)
    for d in range(1, nx):
        ones[d - 1].wait_recv()
        acc = acc + g1[p.xs(-d)].astype(F32)
    r1[...] = acc
    g2[0] = r1[:, row(1 - p.y, cut)].astype(BF16)
    two = p.send(g2.at[0], g2.at[1], p.at(p.x, p.z, 1 - p.y), p.slot())
    two.wait_recv()
    acc = r1[:, row(p.y, cut)] + g2[1].astype(F32)
    r2[...] = acc.astype(BF16)
    zbase = p.slot(nz)
    fbase = p.slot(2 * nx)
    piece = p.x * 2 + p.y

    def up(d, slot):
        return p.copy(r2, g3.at[d], p.at(p.x, 0, p.y), slot)

    def home(d, slot):
        return p.copy(r3, g4.at[d], 0, slot)

    three = up(p.z, zbase + p.z)
    four = home(piece, fbase + piece)

    @pl.when(p.z != 0)
    def _():
        three.start()

    @pl.when(p.z == 0)
    def _():
        for d in range(1, nz):
            up(d, zbase + d).wait_recv()
        tally = acc
        for d in range(1, nz):
            tally = tally + g3[d].astype(F32)
        r3[...] = tally

        @pl.when(p.me != 0)
        def _():
            four.start()

    to_right.wait_recv()
    to_left.wait_recv()
    tot[...] = tot[...] + in_l[...].astype(F32) + in_r[...].astype(F32)

    @pl.when(p.me == 0)
    def _():
        for d in range(1, 2 * nx):
            home(d, fbase + d).wait_recv()
        tot[:, pl.ds(0, cut)] = tot[:, pl.ds(0, cut)] + r3[...]
        for d in range(1, 2 * nx):
            at = pl.ds(d * cut, cut)
            tot[:, at] = tot[:, at] + g4[d]

    @pl.when(p.z != 0)
    def _():
        three.wait_send()

    @pl.when((p.z == 0) & (p.me != 0))
    def _():
        four.wait_send()

    p.drain()


def update_kernel(
    n, hop, scale, vt, tt, wk, weight, ig, nw,
    vt4, igs, dsend, drecv, own, ys, yr, us, ur, send_sem, recv_sem,
):
    p = Place(n, send_sem, recv_sem)
    nx, nz = p.nx, p.nz
    width = tt.shape[2]
    deep = width // nz
    p.greet(near=False, rep=hop)
    base = p.slot(nx)
    sent = [p.send(vt, vt4.at[p.x], p.at(p.xs(d), p.z, p.y), base + d) for d in range(1, nx)]
    vt4[p.x] = vt[...]
    for made in sent:
        made.wait_recv()
    grads = vt4[...].reshape(nx * BLOCK_TOKENS, vt.shape[1])
    tn = (((0,), (0,)), ((), ()))

    def change(block):
        rows = tt[:, :, pl.ds(pl.multiple_of(block * deep, deep), deep)]
        rows = rows.reshape(nx * BLOCK_TOKENS, deep)
        return lax.dot_general(rows, grads, tn, preferred_element_type=F32) * scale

    zbase = p.slot(nz)
    zs = []
    for d in range(1, nz):
        to = p.zs(d)
        part = change(to).astype(BF16)
        dsend[to] = part.reshape(dsend.shape[1:])
        zs.append(p.send(dsend.at[to], drecv.at[p.z], p.at(p.x, to, p.y), zbase + d))
    own[...] = change(p.z).reshape(own.shape)
    ibase = p.slot(nx)
    whole = wk[...].reshape(width, wk.shape[2])
    nt = (((1,), (1,)), ((), ()))

    def back(which):
        return lax.dot_general(vt4[which], whole, nt, preferred_element_type=F32) * scale

    here = pl.ds(pl.multiple_of(p.x * width, width), width)
    backs = []
    for d in range(1, nx):
        to = p.xs(d)
        igs[to] = back(to).astype(BF16)
        backs.append(p.send(igs.at[to], ig.at[:, here], p.at(to, p.z, p.y), ibase + d))
    ig[:, here] = back(p.x).astype(BF16)
    for made in zs:
        made.wait_recv()
    acc = own[...]
    for d in range(1, nz):
        acc = acc + drecv[p.zs(-d)].astype(F32)
    own[...] = acc
    ys[...] = own[1 - p.y].astype(BF16)
    yc = p.send(ys, yr, p.at(p.x, p.z, 1 - p.y), p.slot())
    yc.wait_recv()
    updated = weight[...] - LEARN_RATE * (own[p.y] + yr[...].astype(F32))
    us[...] = updated.astype(BF16)
    reps = lax.axis_size("rep")
    rc = p.send(us, ur, lax.rem(lax.axis_index("rep") + hop, reps), p.slot(), axis="rep")
    rc.wait_recv()
    nw[...] = 0.5 * (updated + ur[...].astype(F32))
    for made in backs:
        made.wait_recv()
    p.drain()


VM = pl.BlockSpec(memory_space=pltpu.VMEM)


def sems(count):
    return [pltpu.SemaphoreType.DMA((count,)), pltpu.SemaphoreType.DMA((count,))]


def params(which, mib=60):
    return pltpu.CompilerParams(
        collective_id=which, has_side_effects=True, vmem_limit_bytes=mib * 2**20
    )


def sds(shape, dtype):
    return jax.ShapeDtypeStruct(shape, dtype)


def swap(a, b, shift, sign, n):
    def branch(c):
        def go(a, b):
            fore = [(i, (i + sign * c) % n) for i in range(n)]
            aft = [(i, (i - sign * (c + 1)) % n) for i in range(n)]
            return lax.ppermute(a, "seq", fore), lax.ppermute(b, "seq", aft)
        return go

    def pick(low, high):
        if high - low == 1:
            return branch(low)
        mid = (low + high) // 2
        one, two = pick(low, mid), pick(mid, high)
        return lambda a, b: lax.cond(shift < mid, one, two, a, b)

    return pick(1, n // 2)(a, b)


def shards(inputs, queries, key_heads, cotangent, value_weight, random_blocks):
    n = lax.axis_size("seq")
    nx, nz = grid_of(n)
    tokens, query, key = inputs[0], queries[0], key_heads[0]
    upstream, weight = cotangent[0], value_weight[0]
    rows, model = tokens.shape
    kvw = key.shape[1]
    qw = query.shape[1]
    deep = weight.shape[0]
    scale = model ** -0.5
    weight_low = weight.astype(BF16)
    offset = lax.rem(n - random_blocks[0, 0], n)
    shift = jnp.minimum(offset, n - 1 - offset)

    kv, wk, tt = pl.pallas_call(
        functools.partial(gather_kernel, n, scale),
        out_shape=(
            sds((4, 2, rows, kvw), BF16),
            sds((2 * nz, deep, kvw), BF16),
            sds((nx, rows, model // nx), BF16),
        ),
        in_specs=[VM] * 3,
        out_specs=(VM,) * 3,
        scratch_shapes=[
            pltpu.VMEM((nx, rows, kvw), BF16),
            pltpu.VMEM((nx, rows, kvw), BF16),
            *sems(96),
        ],
        compiler_params=params(0),
        name="gather",
    )(tokens, key, weight_low)

    pair = kv[1]
    ra, rb = swap(pair, pair, shift, 1, n)

    cut = rows // nx // 2
    dq, tot, cha, chb = pl.pallas_call(
        functools.partial(attend_kernel, n),
        out_shape=(
            sds((rows, qw), BF16),
            sds((2, rows, kvw), F32),
            sds((2, rows, kvw), BF16),
            sds((2, rows, kvw), BF16),
        ),
        in_specs=[VM] * 5,
        out_specs=(VM,) * 4,
        scratch_shapes=[
            pltpu.VMEM((6, rows, kvw), BF16),
            pltpu.VMEM((6, rows, kvw), BF16),
            pltpu.VMEM((GROUP * rows, HD), BF16),
            pltpu.VMEM((GROUP * rows, HD), BF16),
            pltpu.VMEM((6, rows, GROUP * rows), F32),
            pltpu.VMEM((6, rows, GROUP * rows), F32),
            pltpu.VMEM((6, rows, GROUP * rows), BF16),
            *[pltpu.VMEM((2, rows, kvw), BF16)] * 5,
            pltpu.VMEM((nx, 2, 2 * cut, kvw), BF16),
            pltpu.VMEM((2, 2 * cut, kvw), F32),
            pltpu.VMEM((2, 2, cut, kvw), BF16),
            pltpu.VMEM((2, cut, kvw), BF16),
            pltpu.VMEM((nz, 2, cut, kvw), BF16),
            pltpu.VMEM((2, cut, kvw), F32),
            pltpu.VMEM((2 * nx, 2, cut, kvw), F32),
            *sems(32),
        ],
        compiler_params=params(1),
        name="attend",
    )(query, upstream, kv, ra, rb)

    ba, bb = swap(cha, chb, shift, -1, n)
    tot = tot + ba.astype(F32) + bb.astype(F32)
    key_grad = tot[0].astype(BF16)
    value_total = tot[1].astype(BF16)

    reps = lax.axis_size("rep")
    hop = 2 ** (STEP % (reps.bit_length() - 1))
    input_grad, new_weight = pl.pallas_call(
        functools.partial(update_kernel, n, hop, scale),
        out_shape=(sds((rows, model), BF16), sds((deep, kvw), F32)),
        in_specs=[VM] * 4,
        out_specs=(VM,) * 2,
        scratch_shapes=[
            pltpu.VMEM((nx, rows, kvw), BF16),
            pltpu.VMEM((nx, rows, model // nx), BF16),
            pltpu.VMEM((nz, 2, deep, kvw), BF16),
            pltpu.VMEM((nz, 2, deep, kvw), BF16),
            pltpu.VMEM((2, deep, kvw), F32),
            *[pltpu.VMEM((deep, kvw), BF16)] * 4,
            *sems(32),
        ],
        compiler_params=params(2),
        name="update",
    )(value_total, tt, wk, weight)
    return input_grad[None], dq[None], key_grad[None], new_weight[None]


def solution(mesh):
    p3 = P("rep", "seq", None)
    return jax.shard_map(
        shards,
        mesh=mesh,
        in_specs=(p3,) * 5 + (P(),),
        out_specs=(p3,) * 4,
        check_vma=False,
    )
```

time: 2110 us -> 309 us (0.15)
  waiting for transfers between devices: 1920 us -> 28.7 us
  Pallas kernels: 0 us -> 200 us
  starting transfers between devices: 93.6 us -> 34.1 us
  loops' own time: 0 us -> 33.4 us
  local copies, waits for them, and re-layouts: 38.4 us -> 5.95 us
  matrix products: 25.7 us -> 0 us
    psum x2 -> x0, waiting for transfers between devices: 1280 us -> none  [the longest x1 664 us: shards(): global_sum = lax.psum(jnp.sum(changes[:, 3], axis=0), 'seq')]
    reduce_scatter x1 -> x0, waiting for transfers between devices: 373 us -> none  [shards(): lax.psum_scatter(lax.dot_general(tokens, value_total, contract_rows, pref...]
    pallas_call x0 -> x3, Pallas kernels: none -> 200 us  [the longest x1 70.1 us: shards(): pl.pallas_call(functools.partial(update_kernel, n, hop, scale), out_shape...]
    all_gather x1 -> x0, waiting for transfers between devices: 131 us -> none  [shards(): whole_weight = lax.all_gather(weight_low, 'seq', axis=0, tiled=True)]
    ppermute x17 -> x4, waiting for transfers between devices: 135 us -> 28.7 us  [go(): return (lax.ppermute(a, 'seq', fore), lax.ppermute(b, 'seq', aft))]
    ppermute x17 -> x4, starting transfers between devices: 93.5 us -> 34.1 us  [go(): return (lax.ppermute(a, 'seq', fore), lax.ppermute(b, 'seq', aft))]
    another operation x0 -> x6, loops' own time: none -> 32.5 us  [pick(): return lambda a, b: lax.cond(shift < mid, one, two, a, b)]
    dot_general x9 -> x0, matrix products: 25.7 us -> none  [the longest x1 4.64 us: shards(): lax.dot_general(value_total, whole_weight, contract_cols, preferred_eleme...]
  transfers between devices with their start and end apart: 21 -> 4, of which waited for: 16 -> 3; matrix products, arithmetic and copies ran while one was open for 1% -> 0% of each run, Pallas kernels for 0% -> 0%
where the time goes in v1:
time: 309 us; the launch traced here: 307 us
  Pallas kernels  200 us (65%)
  starting transfers between devices  34.1 us (11%)
  loops' own time  33.4 us (11%)
  waiting for transfers between devices  28.7 us (9%)
  local copies, waits for them, and re-layouts  5.95 us (2%)
    pallas_call x1, Pallas kernels, shards(): pl.pallas_call(functools.partial(update_kernel, n, hop, scale), out_shape...  70.1 us
    pallas_call x1, Pallas kernels, shards(): pl.pallas_call(functools.partial(attend_kernel, n), out_shape=(sds((rows,...  65.1 us
    pallas_call x1, Pallas kernels, shards(): pl.pallas_call(functools.partial(gather_kernel, n, scale), out_shape=(sds...  64.5 us
    ppermute x4, starting transfers between devices, go(): return (lax.ppermute(a, 'seq', fore), lax.ppermute(b, 'seq', aft))  34.1 us
    another operation x6, loops' own time, pick(): return lambda a, b: lax.cond(shift < mid, one, two, a, b)  32.5 us
    ppermute x4, waiting for transfers between devices, go(): return (lax.ppermute(a, 'seq', fore), lax.ppermute(b, 'seq', aft))  28.7 us
  transfers between devices with their start and end apart: 4, of which 3 were waited for; matrix products, arithmetic and copies ran while one was open for 0% of the time, Pallas kernels for 0%

profile of v1, /device:TPU:1, one launch (start us, length us, event | category | flops | bytes accessed | tf_op | source)
XLA Modules:
  0.0 306.5 jit_solution(6091848431540863964)
XLA Ops:
  2.5 1.5 bitcast_convert_fusion.wl
  4.0 64.5 %gather.1 = (bf16[4,2,128,512]{3,2,1,0:T(8,128)(2,1)S(1)}, bf16[16,64,512]{2,1,0:T(8,128)(2,1)}, bf16[4,128,1024]{2,1,0:T(8,128)(2,1)}) custom-call(bf16[128,4096]{1,0:T(8,128)(2,1)} %bitcast.28, bf16[128,512]{1,0:T(8,128)(2,1)} %bitcast.34, bf16[64,512]{1,0:T(8,128)(2,1)} %bitcast_convert_fusion.wl), custom_call_target="tpu_custom_call" | custom-call | tf_op jit(solution)/shard_map/gather/pallas_call | solution.py:548
  68.6 57.9 %conditional.60 = ((bf16[2,128,512]{2,1,0:T(8,128)(2,1)}, bf16[2,128,512]{2,1,0:T(8,128)(2,1)})) conditional(s32[]{:T(128)} %convert_element_type.313, (s32[]{:T(128)}, bf16[4,2,128,512]{3,2,1,0:T(8,128)(2,1)S(1)}) %tuple.480, (s32[]{:T(128)}, bf16[4,2,128,512]{3,2,1,0:T(8,128)(2,1)S(1)}) %tuple.480), branch_computations={%region_0.0_spmd, %region_31.0_spmd} | conditional | flops 8 | bytes 2621616 | solution.py:529
  78.1 38.4 %conditional.28 = ((bf16[2,128,512]{2,1,0:T(8,128)(2,1)}, bf16[2,128,512]{2,1,0:T(8,128)(2,1)})) conditional(s32[]{:T(128)} %convert_element_type.247, (s32[]{:T(128)}, bf16[4,2,128,512]{3,2,1,0:T(8,128)(2,1)S(1)}) %param.59, (s32[]{:T(128)}, bf16[4,2,128,512]{3,2,1,0:T(8,128)(2,1)S(1)}) %param.59), branch_computations={%region_32.0_spmd, %region_47.0_spmd} | conditional | flops 6 | bytes 2621602 | solution.py:529
  78.1 37.6 %conditional.21 = ((bf16[2,128,512]{2,1,0:T(8,128)(2,1)}, bf16[2,128,512]{2,1,0:T(8,128)(2,1)})) conditional(s32[]{:T(128)} %convert_element_type.240, (s32[]{:T(128)}, bf16[4,2,128,512]{3,2,1,0:T(8,128)(2,1)S(1)}) %param.45, (s32[]{:T(128)}, bf16[4,2,128,512]{3,2,1,0:T(8,128)(2,1)S(1)}) %param.45), branch_computations={%region_33.0_spmd, %region_40.0_spmd} | conditional | flops 4 | bytes 2621588 | solution.py:529
  78.2 37.5 %conditional.20 = ((bf16[2,128,512]{2,1,0:T(8,128)(2,1)}, bf16[2,128,512]{2,1,0:T(8,128)(2,1)})) conditional(s32[]{:T(128)} %convert_element_type.239, (s32[]{:T(128)}, bf16[2,128,512]{2,1,0:T(8,128)(2,1)S(1)}) %tuple.385, (s32[]{:T(128)}, bf16[2,128,512]{2,1,0:T(8,128)(2,1)S(1)}) %tuple.385), branch_computations={%region_41.0_spmd, %region_44.0_spmd} | conditional | flops 2 | bytes 2097270 | solution.py:529
  78.2 37.5 %conditional.19 = (bf16[2,128,512]{2,1,0:T(8,128)(2,1)}, bf16[2,128,512]{2,1,0:T(8,128)(2,1)}) conditional(s32[]{:T(128)} %convert_element_type.238, bf16[2,128,512]{2,1,0:T(8,128)(2,1)S(1)} %get-tuple-element.610, bf16[2,128,512]{2,1,0:T(8,128)(2,1)S(1)} %get-tuple-element.610), branch_computations={%region_45.0_spmd, %region_46.0_spmd} | conditional | bytes 2097248 | solution.py:529
  78.2 16.6 %collective-permute-start.45 = (bf16[2,128,512]{2,1,0:T(8,128)(2,1)S(1)}, bf16[2,128,512]{2,1,0:T(8,128)(2,1)}, u32[]{:S(2)}, u32[]{:S(2)}) collective-permute-start(bf16[2,128,512]{2,1,0:T(8,128)(2,1)S(1)} %param.41), channel_id=1, source_target_pairs={{0,54},{1,55},{2,56},{3,57},{4,58},{5,59},{6,60},{7,61},{8,62},{9,... | collective-permute-start | bytes 786440 | tf_op jit(solution)/shard_map/cond/branch_1_fun/cond/branch_0_fun/cond/branch_1_fun/cond/branch_1_fun/cond/branch_0_fun/ppermute | solution.py:521
  94.8 8.7 %collective-permute-start.44 = (bf16[2,128,512]{2,1,0:T(8,128)(2,1)S(1)}, bf16[2,128,512]{2,1,0:T(8,128)(2,1)}, u32[]{:S(2)}, u32[]{:S(2)}) collective-permute-start(bf16[2,128,512]{2,1,0:T(8,128)(2,1)S(1)} %param.41), channel_id=1, source_target_pairs={{0,9},{1,10},{2,11},{3,12},{4,13},{5,14},{6,15},{7,16},{8,17},{9,1... | collective-permute-start | bytes 786440 | tf_op jit(solution)/shard_map/cond/branch_1_fun/cond/branch_0_fun/cond/branch_1_fun/cond/branch_1_fun/cond/branch_0_fun/ppermute | solution.py:521
  103.5 12.2 %collective-permute-done.45 = bf16[2,128,512]{2,1,0:T(8,128)(2,1)} collective-permute-done((bf16[2,128,512]{2,1,0:T(8,128)(2,1)S(1)}, bf16[2,128,512]{2,1,0:T(8,128)(2,1)}, u32[]{:S(2)}, u32[]{:S(2)}) %collective-permute-start.45) | collective-permute-done | bytes 262176 | tf_op jit(solution)/shard_map/cond/branch_1_fun/cond/branch_0_fun/cond/branch_1_fun/cond/branch_1_fun/cond/branch_0_fun/ppermute | solution.py:521
  126.6 65.1 %attend.1 = (bf16[128,2048]{1,0:T(8,128)(2,1)}, f32[2,128,512]{2,1,0:T(8,128)}, bf16[2,128,512]{2,1,0:T(8,128)(2,1)S(1)}, bf16[2,128,512]{2,1,0:T(8,128)(2,1)S(1)}) custom-call(bf16[128,2048]{1,0:T(8,128)(2,1)} %bitcast.30, bf16[128,2048]{1,0:T(8,128)(2,1)} %bitcast.31, bf16[4,2,128,512]{3,2,1,0:T(8,128)(2,1)S(1)} %get-tuple-element.796.kv, ...), custom_call_target="tpu_custom_call" | custom-call | tf_op jit(solution)/shard_map/attend/pallas_call | solution.py:570
  191.6 38.3 %conditional.61 = ((bf16[2,128,512]{2,1,0:T(8,128)(2,1)}, bf16[2,128,512]{2,1,0:T(8,128)(2,1)})) conditional(s32[]{:T(128)} %convert_element_type.313, (s32[]{:T(128)}, bf16[2,128,512]{2,1,0:T(8,128)(2,1)S(1)}, bf16[2,128,512]{2,1,0:T(8,128)(2,1)S(1)}) %tuple.481, (s32[]{:T(128)}, bf16[2,128,512]{2,1,0:T(8,128)(2,1)S(1)}, ...), branch_computations={%region_60.0_spmd, %region_91.0_spmd} | conditional | flops 8 | bytes 2097344 | solution.py:529
  201.0 26.3 %conditional.90 = ((bf16[2,128,512]{2,1,0:T(8,128)(2,1)}, bf16[2,128,512]{2,1,0:T(8,128)(2,1)})) conditional(s32[]{:T(128)} %convert_element_type.308, (s32[]{:T(128)}, bf16[2,128,512]{2,1,0:T(8,128)(2,1)S(1)}, bf16[2,128,512]{2,1,0:T(8,128)(2,1)S(1)}) %param.119, (s32[]{:T(128)}, bf16[2,128,512]{2,1,0:T(8,128)(2,1)S(1)}, ...), branch_computations={%region_92.0_spmd, %region_107.0_spmd} | conditional | flops 6 | bytes 2097330
  201.0 25.4 %conditional.83 = ((bf16[2,128,512]{2,1,0:T(8,128)(2,1)}, bf16[2,128,512]{2,1,0:T(8,128)(2,1)})) conditional(s32[]{:T(128)} %convert_element_type.293, (s32[]{:T(128)}, bf16[2,128,512]{2,1,0:T(8,128)(2,1)S(1)}, bf16[2,128,512]{2,1,0:T(8,128)(2,1)S(1)}) %param.105, (s32[]{:T(128)}, bf16[2,128,512]{2,1,0:T(8,128)(2,1)S(1)}, ...), branch_computations={%region_93.0_spmd, %region_100.0_spmd} | conditional | flops 4 | bytes 2097300
  201.0 25.4 %conditional.82 = ((bf16[2,128,512]{2,1,0:T(8,128)(2,1)}, bf16[2,128,512]{2,1,0:T(8,128)(2,1)})) conditional(s32[]{:T(128)} %convert_element_type.292, (s32[]{:T(128)}, bf16[2,128,512]{2,1,0:T(8,128)(2,1)S(1)}, bf16[2,128,512]{2,1,0:T(8,128)(2,1)S(1)}) %param.104, (s32[]{:T(128)}, bf16[2,128,512]{2,1,0:T(8,128)(2,1)S(1)}, ...), branch_computations={%region_101.0_spmd, %region_104.0_spmd} | conditional | flops 2 | bytes 2097286
  201.0 25.4 %conditional.81 = (bf16[2,128,512]{2,1,0:T(8,128)(2,1)}, bf16[2,128,512]{2,1,0:T(8,128)(2,1)}) conditional(s32[]{:T(128)} %convert_element_type.289, (bf16[2,128,512]{2,1,0:T(8,128)(2,1)S(1)}, bf16[2,128,512]{2,1,0:T(8,128)(2,1)S(1)}) %tuple.454, (bf16[2,128,512]{2,1,0:T(8,128)(2,1)S(1)}, bf16[2,128,512]{2,1,0:T(8,128)(2,1)S(1)}) %tuple.454), branch_computations={%region_105.0_spmd, %region_106.0_spmd} | conditional | bytes 2097248
  201.0 3.2 %collective-permute-start.106 = (bf16[2,128,512]{2,1,0:T(8,128)(2,1)S(1)}, bf16[2,128,512]{2,1,0:T(8,128)(2,1)}, u32[]{:S(2)}, u32[]{:S(2)}) collective-permute-start(bf16[2,128,512]{2,1,0:T(8,128)(2,1)S(1)} %get-tuple-element.733), channel_id=1, source_target_pairs={{0,55},{1,56},{2,57},{3,58},{4,59},{5,60},{6,61},{7,62},{8,63},{9,... | collective-permute-start | bytes 786440 | tf_op jit(solution)/shard_map/cond/branch_1_fun/cond/branch_0_fun/cond/branch_1_fun/cond/branch_1_fun/cond/branch_0_fun/ppermute | solution.py:521
  204.2 5.6 %collective-permute-start.107 = (bf16[2,128,512]{2,1,0:T(8,128)(2,1)S(1)}, bf16[2,128,512]{2,1,0:T(8,128)(2,1)}, u32[]{:S(2)}, u32[]{:S(2)}) collective-permute-start(bf16[2,128,512]{2,1,0:T(8,128)(2,1)S(1)} %get-tuple-element.734), channel_id=1, source_target_pairs={{0,10},{1,11},{2,12},{3,13},{4,14},{5,15},{6,16},{7,17},{8,18},{9,... | collective-permute-start | bytes 786440 | tf_op jit(solution)/shard_map/cond/branch_1_fun/cond/branch_0_fun/cond/branch_1_fun/cond/branch_1_fun/cond/branch_0_fun/ppermute | solution.py:521
  209.8 15.2 %collective-permute-done.106 = bf16[2,128,512]{2,1,0:T(8,128)(2,1)} collective-permute-done((bf16[2,128,512]{2,1,0:T(8,128)(2,1)S(1)}, bf16[2,128,512]{2,1,0:T(8,128)(2,1)}, u32[]{:S(2)}, u32[]{:S(2)}) %collective-permute-start.106) | collective-permute-done | bytes 262176 | tf_op jit(solution)/shard_map/cond/branch_1_fun/cond/branch_0_fun/cond/branch_1_fun/cond/branch_1_fun/cond/branch_0_fun/ppermute | solution.py:521
  225.0 1.4 collective-permute-done.107
  230.0 1.1 fusion.1
  231.9 70.1 %update.1 = (bf16[128,4096]{1,0:T(8,128)(2,1)}, f32[64,512]{1,0:T(8,128)}) custom-call(bf16[128,512]{1,0:T(8,128)(2,1)} %get-tuple-element.959.vt, bf16[4,128,1024]{2,1,0:T(8,128)(2,1)} %get-tuple-element.804.tt, bf16[16,64,512]{2,1,0:T(8,128)(2,1)} %get-tuple-element.805.wk, f32[64,512]{1,0:T(8,128)} %bitcast.32), custom_call_target="tpu_custom_call" | custom-call | tf_op jit(solution)/shard_map/update/pallas_call | solution.py:609
  301.9 2.3 copy.253
  304.3 0.8 copy.254
  (13 shorter events, 2.8 us)
Async XLA Ops:
  0.6 0.7 copy-start.3
  78.2 37.5 %collective-permute-start.45 = (bf16[2,128,512]{2,1,0:T(8,128)(2,1)S(1)}, bf16[2,128,512]{2,1,0:T(8,128)(2,1)}, u32[]{:S(2)}, u32[]{:S(2)}) collective-permute-start(bf16[2,128,512]{2,1,0:T(8,128)(2,1)S(1)} %param.41), channel_id=1, source_target_pairs={{0,54},{1,55},{2,56},{3,57},{4,58},{5,59},{6,60},{7,61},{8,62},{9,... | collective-permute-start | bytes 786440 | tf_op jit(solution)/shard_map/cond/branch_1_fun/cond/branch_0_fun/cond/branch_1_fun/cond/branch_1_fun/cond/branch_0_fun/ppermute | solution.py:521
  94.8 20.9 %collective-permute-start.44 = (bf16[2,128,512]{2,1,0:T(8,128)(2,1)S(1)}, bf16[2,128,512]{2,1,0:T(8,128)(2,1)}, u32[]{:S(2)}, u32[]{:S(2)}) collective-permute-start(bf16[2,128,512]{2,1,0:T(8,128)(2,1)S(1)} %param.41), channel_id=1, source_target_pairs={{0,9},{1,10},{2,11},{3,12},{4,13},{5,14},{6,15},{7,16},{8,17},{9,1... | collective-permute-start | bytes 786440 | tf_op jit(solution)/shard_map/cond/branch_1_fun/cond/branch_0_fun/cond/branch_1_fun/cond/branch_1_fun/cond/branch_0_fun/ppermute | solution.py:521
  191.6 38.4 %copy-start.1 = (f32[2,128,512]{2,1,0:T(8,128)S(1)}, f32[2,128,512]{2,1,0:T(8,128)}, u32[]{:S(2)}) copy-start(f32[2,128,512]{2,1,0:T(8,128)} %get-tuple-element.799) | copy-start | bytes 1572868
  201.0 23.9 %collective-permute-start.106 = (bf16[2,128,512]{2,1,0:T(8,128)(2,1)S(1)}, bf16[2,128,512]{2,1,0:T(8,128)(2,1)}, u32[]{:S(2)}, u32[]{:S(2)}) collective-permute-start(bf16[2,128,512]{2,1,0:T(8,128)(2,1)S(1)} %get-tuple-element.733), channel_id=1, source_target_pairs={{0,55},{1,56},{2,57},{3,58},{4,59},{5,60},{6,61},{7,62},{8,63},{9,... | collective-permute-start | bytes 786440 | tf_op jit(solution)/shard_map/cond/branch_1_fun/cond/branch_0_fun/cond/branch_1_fun/cond/branch_1_fun/cond/branch_0_fun/ppermute | solution.py:521
  204.2 22.1 %collective-permute-start.107 = (bf16[2,128,512]{2,1,0:T(8,128)(2,1)S(1)}, bf16[2,128,512]{2,1,0:T(8,128)(2,1)}, u32[]{:S(2)}, u32[]{:S(2)}) collective-permute-start(bf16[2,128,512]{2,1,0:T(8,128)(2,1)S(1)} %get-tuple-element.734), channel_id=1, source_target_pairs={{0,10},{1,11},{2,12},{3,13},{4,14},{5,15},{6,16},{7,17},{8,18},{9,... | collective-permute-start | bytes 786440 | tf_op jit(solution)/shard_map/cond/branch_1_fun/cond/branch_0_fun/cond/branch_1_fun/cond/branch_1_fun/cond/branch_0_fun/ppermute | solution.py:521
  301.9 2.4 copy-start
  304.3 1.0 copy-start.2
